TPU v7x, 256 devices: a whole 4x4x8 slice. The times are simulated.
256 devices in a mesh: src: 32 (over z_hi, x, core), tgt: 8 (over y, z_lo).
Axes of the slice: x: 4, y: 4, z: 8 (z_hi: 4, z_lo: 2; z = z_hi * 2 + z_lo), core: 2. Of those that a mesh axis runs over, the one named last changes fastest.
Arguments:
- upstream: bfloat16 [256, 128, 324], P('src'), may hold values from -6 to 6
- centers: int32 [2, 256, 128], P(None, 'src'), may hold values from -4 to 259, as said below
- post_relu: bfloat16 [256, 128, 128], P('src'), as said below
- conv_input: bfloat16 [256, 128, 128], P(('src', 'tgt')), may hold values from -6 to 6
- target_feats: bfloat16 [64, 256, 256], P('tgt'), may hold values from -6 to 6
- out_weight: bfloat16 [128, 256], replicated, may hold values from -0.5 to 0.5
- conv_weight: bfloat16 [3, 3, 128, 128], replicated, may hold values from -0.1875 to 0.1875
Outputs:
- tgt_grad: bfloat16 [64, 256, 256], P('tgt', 'src')
- act_grad: bfloat16 [256, 128, 128], P(('src', 'tgt'))
- out_wgrad: float32 [128, 256], replicated
- conv_wgrad: float32 [3, 3, 128, 128], replicated
Inputs may be any that keep to these rules, and one draw needn't show every extreme that they name: centers[0] is a target row from -4 to 67 and centers[1] a target column from -4 to 259; windows may reach outside the target image. `post_relu`: entries are zero or positive.
All inputs are finite; a program needn't handle non-finite values.
Results may differ from a plain program's by a relative error of at most 0.0064.
Values may be sent and summed in bfloat16 or wider, within the bound.
No kernel may reach another device: no remote copies, remote signals or barrier semaphores. Data moves between devices by JAX's collectives and lax.ppermute only.
A program may use at most 64 MiB of HBM per device.

v0:
```python
import math
import jax
import jax.numpy as jnp
from jax import lax
from jax.sharding import PartitionSpec as P


def padded_2(array, sides, width):
    for axis, dim in sides:
        devices, length = (lax.axis_size(axis), array.shape[dim])
        up = [(i, (i + 1) % devices) for i in range(devices - 1)]
        down = [(j, i) for i, j in up]
        last = lax.slice_in_dim(array, length - width, length, axis=dim)
        first = lax.slice_in_dim(array, 0, width, axis=dim)
        before = lax.ppermute(last, axis, up)
        after = lax.ppermute(first, axis, down)
        array = jnp.concatenate([before, array, after], axis=dim)
    return array


def corr_block(center_rows, center_cols, grad_rows, row_start, row_total, col_total):
    source_total = grad_rows.shape[0]
    row_ids = row_start + jnp.arange(row_total, dtype=jnp.int32)
    col_ids = jnp.arange(col_total, dtype=jnp.int32)
    offsets = jnp.arange(9, dtype=jnp.int32)
    row_parts = []
    col_parts = []
    for level_no in range(4):
        level_step = 2**level_no
        row_off = (
            jnp.floor_divide(row_ids, level_step)[None, :]
            - jnp.floor_divide(center_rows, level_step)[:, None]
            + 4
        )
        col_off = (
            jnp.floor_divide(col_ids, level_step)[None, :]
            - jnp.floor_divide(center_cols, level_step)[:, None]
            + 4
        )
        row_hot = jnp.where(
            row_off[:, None, :] == offsets[None, :, None], 0.25**level_no, 0.0
        ).astype(jnp.float32)
        col_hot = jnp.where(col_off[:, None, :] == offsets[None, :, None], 1.0, 0.0).astype(
            jnp.float32
        )
        level_grads = (
            grad_rows[:, 81 * level_no : 81 * (level_no + 1)]
            .astype(jnp.float32)
            .reshape(source_total, 9, 9)
        )
        row_parts.append(row_hot)
        col_parts.append(jnp.einsum("sab,sbx->sax", level_grads, col_hot))
    row_table = jnp.concatenate(row_parts, axis=1)
    col_table = jnp.concatenate(col_parts, axis=1)
    return jnp.einsum("say,sax->syx", row_table, col_table).astype(jnp.bfloat16)


def hidden_grads(src_grad, relu_rows, out_weight):
    hidden = jnp.einsum("rwd,cd->rwc", src_grad, out_weight, preferred_element_type=jnp.float32)
    block_grad = jnp.where(relu_rows > 0, hidden, 0.0).astype(jnp.bfloat16)
    out_term = jnp.einsum("rwc,rwd->cd", relu_rows, src_grad, preferred_element_type=jnp.float32)
    return (block_grad, out_term)


def conv_back(grad_pad, inputs, kernel):
    row_total = inputs.shape[0]
    width_total = inputs.shape[1]
    padded = jnp.pad(grad_pad, ((0, 0), (1, 1), (0, 0)))
    act_sum = jnp.zeros(inputs.shape, jnp.float32)
    tap_grads = []
    for row_tap in range(3):
        for col_tap in range(3):
            window = padded[
                2 - row_tap : 2 - row_tap + row_total, 2 - col_tap : 2 - col_tap + width_total
            ]
            act_sum = act_sum + jnp.einsum(
                "rwo,io->rwi", window, kernel[row_tap, col_tap], preferred_element_type=jnp.float32
            )
            tap_grads.append(
                jnp.einsum("rwi,rwo->io", inputs, window, preferred_element_type=jnp.float32)
            )
    channels = inputs.shape[2]
    return (act_sum, jnp.stack(tap_grads).reshape(3, 3, channels, channels))


def body(upstream, centers, post_relu, conv_input, target_feats, out_weight, conv_weight):
    src_rows, src_width, lookups = upstream.shape
    tgt_rows, tgt_width, feat_width = target_feats.shape
    channels = post_relu.shape[2]
    src_devices = lax.axis_size("src")
    tgt_devices = lax.axis_size("tgt")
    row_first = lax.axis_index("tgt") * tgt_rows
    inv_root = 1.0 / math.sqrt(feat_width)
    source_total = src_rows * src_width
    flat_grads = upstream.reshape(source_total, lookups)
    flat_rows = centers[0].reshape(source_total)
    flat_cols = centers[1].reshape(source_total)
    block_size = math.gcd(256, source_total)

    def build_block(block_no):
        first_row = block_no * block_size
        return corr_block(
            lax.dynamic_slice_in_dim(flat_rows, first_row, block_size),
            lax.dynamic_slice_in_dim(flat_cols, first_row, block_size),
            lax.dynamic_slice_in_dim(flat_grads, first_row, block_size, 0),
            row_first,
            tgt_rows,
            tgt_width,
        )

    corr_grad = lax.map(build_block, jnp.arange(source_total // block_size, dtype=jnp.int32))
    corr_grad = corr_grad.reshape(source_total, tgt_rows, tgt_width)
    corr_flat = corr_grad.reshape(source_total, tgt_rows * tgt_width)
    src_feats = jnp.dot(
        post_relu.reshape(source_total, channels), out_weight, preferred_element_type=jnp.float32
    ).astype(jnp.bfloat16)
    flat_targets = target_feats.reshape(tgt_rows * tgt_width, feat_width)
    corr_piece = lax.slice_in_dim(
        corr_grad, 0, tgt_width // src_devices * lax.axis_size("src"), axis=2
    )
    target_share = lax.psum_scatter(
        jnp.einsum("syc,sd->cyd", corr_piece, src_feats, preferred_element_type=jnp.float32)
        * inv_root,
        "src",
        scatter_dimension=0,
        tiled=True,
    )
    tgt_grad = jnp.transpose(target_share, (1, 0, 2)).astype(jnp.bfloat16)
    tile_rows = src_rows // tgt_devices
    src_partial = jnp.dot(corr_flat, flat_targets, preferred_element_type=jnp.float32) * inv_root
    src_total = lax.psum(src_partial, "tgt")
    src_grad = src_total.reshape(src_rows, src_width, feat_width).astype(jnp.bfloat16)
    block_grad, out_term = hidden_grads(src_grad, post_relu, out_weight)
    grad_pad = padded_2(block_grad, (("src", 0),), 1)
    whole_input = lax.all_gather(conv_input, "tgt", axis=0, tiled=True)
    act_sum, conv_term = conv_back(grad_pad, whole_input, conv_weight)
    out_total, conv_total = lax.psum((out_term, conv_term), "src")
    act_grad = lax.dynamic_slice_in_dim(
        act_sum, lax.axis_index("tgt") * tile_rows, tile_rows, 0
    ).astype(jnp.bfloat16)
    row_count = float(src_rows * src_devices)
    return (tgt_grad, act_grad, out_total / row_count, conv_total / row_count)


def solution(mesh):
    placed = (
        P("src", None, None),
        P(None, "src", None),
        P("src", None, None),
        P(("src", "tgt"), None, None),
        P("tgt", None, None),
        P(),
        P(),
    )
    return jax.shard_map(
        body,
        mesh=mesh,
        in_specs=placed,
        out_specs=(P("tgt", "src", None), P(("src", "tgt"), None, None), P(), P()),
        check_vma=False,
    )
```

profile of v0, /device:TPU:8, one launch (start us, length us, event | category | flops | bytes accessed | tf_op | source)
XLA Modules:
  0.0 605.3 jit_solution(13785077860471548321)
XLA Ops:
  7.2 0.8 slice_bitcast_fusion
  8.0 1.1 pad.23
  9.3 84.5 %while.13 = (s32[]{:T(128)}, bf16[4,256,8,256]{3,2,1,0:T(8,128)(2,1)}, s32[]{:T(128)}, s32[4]{0:T(128)S(1)}, s32[1024]{0:T(1024)S(1)}, /*index=5*/bf16[1024,324]...) while((s32[]{:T(128)}, ...), condition=%wide.region_1.2_spmd, body=%wide.region_0.1_spmd.sunk | while | flops 104745304 | bytes 30385264 | solution.py:111
  9.3 0.7 dynamic_slice.64
  11.9 1.0 copy.85
  12.9 2.0 fusion.171
  15.1 1.0 copy.86
  16.1 2.1 fusion.172
  18.3 1.0 copy.88
  19.3 2.0 fusion.174
  21.5 1.0 copy.87
  22.5 0.7 fusion.173
  23.2 0.9 copy-done.8
  24.7 5.7 fusion.175
  30.4 0.7 dynamic_slice.64
  33.0 1.0 copy.85
  34.0 2.0 fusion.171
  36.2 1.0 copy.86
  37.2 2.1 fusion.172
  39.4 1.0 copy.88
  40.4 2.0 fusion.174
  42.6 1.0 copy.87
  43.6 0.7 fusion.173
  44.4 0.9 copy-done.8
  45.9 5.7 fusion.175
  51.6 0.7 dynamic_slice.64
  54.1 1.0 copy.85
  55.1 2.0 fusion.171
  57.3 1.0 copy.86
  58.3 2.1 fusion.172
  60.6 1.0 copy.88
  61.6 2.0 fusion.174
  63.8 1.0 copy.87
  64.8 0.7 fusion.173
  65.5 0.9 copy-done.8
  67.0 5.7 fusion.175
  72.7 0.7 dynamic_slice.64
  75.2 1.0 copy.85
  76.2 2.0 fusion.171
  78.4 1.0 copy.86
  79.4 2.1 fusion.172
  81.7 1.0 copy.88
  82.7 2.0 fusion.174
  84.9 1.0 copy.87
  85.9 0.7 fusion.173
  86.6 0.9 copy-done.8
  88.1 5.7 fusion.175
  93.8 3.7 copy.74
  97.5 1.3 convolution_multiply_fusion
  98.8 75.3 %all-reduce.6 = bf16[1024,256]{1,0:T(8,128)(2,1)S(1)} all-reduce(f32[1024,256]{1,0:T(8,128)S(1)} %convolution_multiply_fusion), channel_id=1, replica_groups=mesh['src'=32,'tgt'=8] {'tgt'}, use_global_device_ids=true, to_apply=%region_3.4 | all-reduce | flops 262144 | bytes 1572864 | tf_op jit(solution)/shard_map/psum | solution.py:131
  174.4 1.3 collective-permute-start
  175.7 1.3 collective-permute-start.1
  177.0 1.0 convolution_bitcast_fusion
  178.0 28.5 %all_gather.3 = bf16[8,128,128]{2,1,0:T(8,128)(2,1)S(1)} all-gather(bf16[1,128,128]{2,1,0:T(8,128)(2,1)S(1)} %copy-done.7), channel_id=1, replica_groups=mesh['src'=32,'tgt'=8] {'tgt'}, dimensions={0}, use_global_device_ids=true | all-gather | bytes 294912 | tf_op jit(solution)/shard_map/all_gather | solution.py:135
  209.2 1.1 copy.58
  210.3 5.6 multiply_bitcast_fusion
  215.9 3.1 copy.47
  221.1 0.7 fusion.89
  221.7 280.7 %all-reduce.5.cloned.1.call-done = (f32[128,256]{0,1:T(8,128)}, f32[3,3,128,128]{3,2,1,0:T(8,128)}) async-done(((f32[128,256]{0,1:T(8,128)}, f32[3,3,128,128]{3,2,1,0:T(8,128)}), (f32[128,256]{0,1:T(8,128)}, f32[3,3,128,128]{3,2,1,0:T(8,128)})) %all-reduce.5.cloned.1.call-update) | async-done | bytes 720912 | tf_op jit(solution)/shard_map/psum | solution.py:137
  502.4 0.9 broadcast_multiply_fusion.1
  503.3 0.8 copy.60
  504.1 1.9 broadcast_multiply_fusion
  506.0 91.0 %reduce-scatter.2.cloned.1.call-done = f32[8,8,256]{2,1,0:T(8,128)} async-done(((f32[256,8,256]{2,1,0:T(8,128)}), f32[8,8,256]{2,1,0:T(8,128)}) %reduce-scatter.2.cloned.1.call-update) | async-done | bytes 65552 | tf_op jit(solution)/shard_map/reduce_scatter | solution.py:121
  597.0 0.8 convert_bitcast_fusion
  (179 shorter events, 14.5 us)
Async XLA Ops:
  7.2 90.3 %copy-start = (bf16[8,256,256]{2,1,0:T(8,128)(2,1)S(1)}, bf16[8,256,256]{2,1,0:T(8,128)(2,1)}, u32[]{:S(2)}) copy-start(bf16[8,256,256]{2,1,0:T(8,128)(2,1)} %param.13) | copy-start | bytes 3145732
  7.2 495.2 %all-reduce.5.cloned.1.call-start = ((), (), s32[]{:S(2)}) async-start(), calls=%async_computation.2 | async-start | bytes 1441792 | tf_op jit(solution)/shard_map/psum | solution.py:137
  9.3 2.5 copy-start.1
  22.5 1.6 copy-start.8
  22.5 2.2 copy-start.9
  24.7 5.7 copy-start.2
  30.4 2.5 copy-start.1
  43.6 1.6 copy-start.8
  43.6 2.2 copy-start.9
  45.9 5.7 copy-start.2
  51.6 2.5 copy-start.1
  64.8 1.6 copy-start.8
  64.8 2.2 copy-start.9
  67.0 5.7 copy-start.2
  72.7 2.5 copy-start.1
  85.9 1.6 copy-start.8
  85.9 2.2 copy-start.9
  88.1 5.7 copy-start.2
  97.5 76.6 %copy-start.3 = (bf16[8,128,128]{2,1,0:T(8,128)(2,1)S(1)}, bf16[8,128,128]{2,1,0:T(8,128)(2,1)}, u32[]{:S(2)}) copy-start(bf16[8,128,128]{2,1,0:T(8,128)(2,1)} %param.11) | copy-start | bytes 786436
  97.5 76.6 %copy-start.5 = (bf16[128,256]{1,0:T(8,128)(2,1)S(1)}, bf16[128,256]{1,0:T(8,128)(2,1)}, u32[]{:S(2)}) copy-start(bf16[128,256]{1,0:T(8,128)(2,1)} %param.14) | copy-start | bytes 196612
  97.5 80.6 %copy-start.7 = (bf16[1,128,128]{2,1,0:T(8,128)(2,1)S(1)}, bf16[1,128,128]{2,1,0:T(8,128)(2,1)}, u32[]{:S(2)}) copy-start(bf16[1,128,128]{2,1,0:T(8,128)(2,1)} %param.12) | copy-start | bytes 98308
  174.4 32.1 %collective-permute-start = (bf16[1,128,128]{2,1,0:T(8,128)(2,1)S(1)}, bf16[1,128,128]{2,1,0:T(8,128)(2,1)S(1)}, u32[]{:S(2)}, u32[]{:S(2)}) collective-permute-start(bf16[1,128,128]{2,1,0:T(8,128)(2,1)S(1)} %get-tuple-element.192), channel_id=1, source_target_pairs={{0,8},{8,16},{16,24},{24,32},{32,40},{40,48},{48,56},{56,64},{64,7... | collective-permute-start | bytes 98312 | tf_op jit(solution)/shard_map/ppermute | solution.py:15
  175.7 30.8 %collective-permute-start.1 = (bf16[1,128,128]{2,1,0:T(8,128)(2,1)S(1)}, bf16[1,128,128]{2,1,0:T(8,128)(2,1)S(1)}, u32[]{:S(2)}, u32[]{:S(2)}) collective-permute-start(bf16[1,128,128]{2,1,0:T(8,128)(2,1)S(1)} %get-tuple-element.193), channel_id=1, source_target_pairs={{8,0},{16,8},{24,16},{32,24},{40,32},{48,40},{56,48},{64,56},{72,6... | collective-permute-start | bytes 98312 | tf_op jit(solution)/shard_map/ppermute | solution.py:16
  206.7 3.6 copy-start.6
  210.2 386.7 %reduce-scatter.2.cloned.1.call-start = ((), (), s32[]{:S(2)}) async-start(), calls=%async_computation.1 | async-start | bytes 2162688 | tf_op jit(solution)/shard_map/reduce_scatter | solution.py:121
  215.9 3.1 copy-start.4
Sparse Core Ops, SparseCore 0:
  210.4 292.0 all-reduce.4
  506.3 90.6 reduce-scatter.1
where the time goes:
time: 606 us; the launch traced here: 605 us
  waiting for transfers between devices  372 us (61%)
  blocking collectives  104 us (17%)
  matrix products  62.9 us (10%)
  local copies, waits for them, and re-layouts  38.5 us (6%)
  between operations  14.3 us (2%)
  other arithmetic  8.06 us (1%)
    psum x1, waiting for transfers between devices, body(): out_total, conv_total = lax.psum((out_term, conv_term), 'src')  281 us
    reduce_scatter x1, waiting for transfers between devices, body(): lax.psum_scatter(jnp.einsum('syc,sd->cyd', corr_piece, src_feats, preferr...  91 us
    psum x1, blocking collectives, body(): src_total = lax.psum(src_partial, 'tgt')  75.3 us
    all_gather x1, blocking collectives, body(): whole_input = lax.all_gather(conv_input, 'tgt', axis=0, tiled=True)  28.5 us
    dot_general x16, matrix products, corr_block(): col_parts.append(jnp.einsum('sab,sbx->sax', level_grads, col_hot))  27.5 us
    dot_general x4, matrix products, corr_block(): return jnp.einsum('say,sax->syx', row_table, col_table).astype(jnp.bfloat16)  22.8 us
    reshape x32, local copies, waits for them, and re-layouts, corr_block(): level_grads = grad_rows[:, 81 * level_no:81 * (level_no + 1)].astype(jnp....  16.4 us
  transfers between devices with their start and end apart: 4, of which 2 were waited for; matrix products, arithmetic and copies ran while one was open for 3% of the time, Pallas kernels for 0%

commit v1 on v0

--- a/solution.py
+++ b/solution.py
@@ -132,7 +132,9 @@
     src_grad = src_total.reshape(src_rows, src_width, feat_width).astype(jnp.bfloat16)
     block_grad, out_term = hidden_grads(src_grad, post_relu, out_weight)
     grad_pad = padded_2(block_grad, (("src", 0),), 1)
-    whole_input = lax.all_gather(conv_input, "tgt", axis=0, tiled=True)
+    whole_input = jnp.concatenate(
+        lax.all_to_all(jnp.stack([conv_input] * lax.axis_size("tgt")), "tgt", 0, 0), axis=0
+    )
     act_sum, conv_term = conv_back(grad_pad, whole_input, conv_weight)
     out_total, conv_total = lax.psum((out_term, conv_term), "src")
     act_grad = lax.dynamic_slice_in_dim(

time: 606 us -> 590 us (0.974)
  blocking collectives: 104 us -> 75 us
  starting transfers between devices: 2.66 us -> 8.9 us
    all_gather x1 -> x0, blocking collectives: 28.5 us -> none  [body(): whole_input = lax.all_gather(conv_input, 'tgt', axis=0, tiled=True)]
    all_to_all x0 -> x1, starting transfers between devices: none -> 6.27 us  [body(): lax.all_to_all(jnp.stack([conv_input] * lax.axis_size('tgt')), 'tgt', 0, 0)]
  transfers between devices with their start and end apart: 4 -> 5, of which waited for: 2 -> 3; matrix products, arithmetic and copies ran while one was open for 3% -> 17% of each run, Pallas kernels for 0% -> 0%
where the time goes in v1:
time: 590 us; the launch traced here: 589 us
  waiting for transfers between devices  376 us (64%)
  blocking collectives  75 us (13%)
  matrix products  63.9 us (11%)
  local copies, waits for them, and re-layouts  40 us (7%)
  between operations  14.3 us (2%)
  starting transfers between devices  8.9 us (2%)
  other arithmetic  8.07 us (1%)
    psum x1, waiting for transfers between devices, body(): out_total, conv_total = lax.psum((out_term, conv_term), 'src')  282 us
    reduce_scatter x1, waiting for transfers between devices, body(): lax.psum_scatter(jnp.einsum('syc,sd->cyd', corr_piece, src_feats, preferr...  91 us
    psum x1, blocking collectives, body(): src_total = lax.psum(src_partial, 'tgt')  75 us
    dot_general x16, matrix products, corr_block(): col_parts.append(jnp.einsum('sab,sbx->sax', level_grads, col_hot))  27.5 us
    dot_general x4, matrix products, corr_block(): return jnp.einsum('say,sax->syx', row_table, col_table).astype(jnp.bfloat16)  22.8 us
    reshape x32, local copies, waits for them, and re-layouts, corr_block(): level_grads = grad_rows[:, 81 * level_no:81 * (level_no + 1)].astype(jnp....  16.4 us
  transfers between devices with their start and end apart: 5, of which 3 were waited for; matrix products, arithmetic and copies ran while one was open for 17% of the time, Pallas kernels for 0%

profile of v1, /device:TPU:8, one launch (start us, length us, event | category | flops | bytes accessed | tf_op | source)
XLA Modules:
  0.0 589.1 jit_solution(11824357642410044804)
XLA Ops:
  7.2 1.6 stack.41
  8.8 6.3 %all-to-all-start = ((bf16[8,1,128,128]{3,2,1,0:T(8,128)(2,1)}), bf16[8,1,128,128]{3,2,1,0:T(8,128)(2,1)S(1)}, u32[]{:S(2)}, u32[]{:S(2)}) async-start(bf16[8,1,128,128]{3,2,1,0:T(8,128)(2,1)} %stack.41), calls=%async_computation.1 | async-start | bytes 524288 | tf_op jit(solution)/shard_map/all_to_all | solution.py:136
  15.0 0.7 slice_bitcast_fusion
  15.7 1.1 pad.23
  17.0 84.5 %while.13 = (s32[]{:T(128)}, bf16[4,256,8,256]{3,2,1,0:T(8,128)(2,1)}, s32[]{:T(128)}, s32[4]{0:T(128)S(1)}, s32[1024]{0:T(1024)S(1)}, /*index=5*/bf16[1024,324]...) while((s32[]{:T(128)}, ...), condition=%wide.region_1.2_spmd, body=%wide.region_0.1_spmd.sunk | while | flops 104745304 | bytes 30385264 | solution.py:111
  17.0 0.7 dynamic_slice.64
  19.6 1.0 copy.85
  20.6 2.0 fusion.171
  22.8 1.0 copy.86
  23.8 2.1 fusion.172
  26.0 1.0 copy.88
  27.0 2.0 fusion.174
  29.2 1.0 copy.87
  30.3 0.7 fusion.173
  31.0 0.9 copy-done.6
  32.5 5.7 fusion.175
  38.2 0.7 dynamic_slice.64
  40.7 1.0 copy.85
  41.7 2.0 fusion.171
  43.9 1.0 copy.86
  44.9 2.1 fusion.172
  47.1 1.0 copy.88
  48.1 2.0 fusion.174
  50.3 1.0 copy.87
  51.4 0.7 fusion.173
  52.1 0.9 copy-done.6
  53.6 5.7 fusion.175
  59.3 0.7 dynamic_slice.64
  61.9 1.0 copy.85
  62.9 2.0 fusion.171
  65.1 1.0 copy.86
  66.1 2.1 fusion.172
  68.3 1.0 copy.88
  69.3 2.0 fusion.174
  71.5 1.0 copy.87
  72.5 0.7 fusion.173
  73.2 0.9 copy-done.6
  74.7 5.7 fusion.175
  83.0 1.0 copy.85
  84.0 2.0 fusion.171
  86.2 1.0 copy.86
  87.2 2.1 fusion.172
  89.4 1.0 copy.88
  90.4 2.0 fusion.174
  92.6 1.0 copy.87
  93.6 0.7 fusion.173
  94.3 0.9 copy-done.6
  95.8 5.7 fusion.175
  101.5 3.7 copy.74
  105.2 2.3 convolution_multiply_fusion
  107.5 75.0 %all-reduce.6 = bf16[1024,256]{1,0:T(8,128)(2,1)S(1)} all-reduce(f32[1024,256]{1,0:T(8,128)} %convolution_multiply_fusion), channel_id=1, replica_groups=mesh['src'=32,'tgt'=8] {'tgt'}, use_global_device_ids=true, to_apply=%region_3.4 | all-reduce | flops 262144 | bytes 1572864 | tf_op jit(solution)/shard_map/psum | solution.py:131
  182.8 1.3 collective-permute-start
  184.1 1.3 collective-permute-start.1
  185.4 1.0 convolution_bitcast_fusion
  186.4 2.5 collective-permute-done.1
  191.6 1.1 copy.58
  192.7 5.5 multiply_bitcast_fusion
  198.3 3.1 copy.47
  204.1 282.2 %all-reduce.5.cloned.1.call-done = (f32[128,256]{0,1:T(8,128)}, f32[3,3,128,128]{3,2,1,0:T(8,128)}) async-done(((f32[128,256]{0,1:T(8,128)}, f32[3,3,128,128]{3,2,1,0:T(8,128)}), (f32[128,256]{0,1:T(8,128)}, f32[3,3,128,128]{3,2,1,0:T(8,128)})) %all-reduce.5.cloned.1.call-update) | async-done | bytes 720912 | tf_op jit(solution)/shard_map/psum | solution.py:139
  486.3 0.9 broadcast_multiply_fusion.1
  487.2 0.8 copy.60
  488.0 1.9 broadcast_multiply_fusion
  489.9 91.0 %reduce-scatter.2.cloned.1.call-done = f32[8,8,256]{2,1,0:T(8,128)} async-done(((f32[256,8,256]{2,1,0:T(8,128)}), f32[8,8,256]{2,1,0:T(8,128)}) %reduce-scatter.2.cloned.1.call-update) | async-done | bytes 65552 | tf_op jit(solution)/shard_map/reduce_scatter | solution.py:121
  580.8 0.8 convert_bitcast_fusion
  (177 shorter events, 15.8 us)
Async XLA Ops:
  7.2 98.0 %copy-start = (bf16[8,256,256]{2,1,0:T(8,128)(2,1)S(1)}, bf16[8,256,256]{2,1,0:T(8,128)(2,1)}, u32[]{:S(2)}) copy-start(bf16[8,256,256]{2,1,0:T(8,128)(2,1)} %param.13) | copy-start | bytes 3145732
  8.8 180.3 %all-to-all-start = ((bf16[8,1,128,128]{3,2,1,0:T(8,128)(2,1)}), bf16[8,1,128,128]{3,2,1,0:T(8,128)(2,1)S(1)}, u32[]{:S(2)}, u32[]{:S(2)}) async-start(bf16[8,1,128,128]{3,2,1,0:T(8,128)(2,1)} %stack.41), calls=%async_computation.1 | async-start | bytes 524288 | tf_op jit(solution)/shard_map/all_to_all | solution.py:136
  15.0 471.2 %all-reduce.5.cloned.1.call-start = ((), (), s32[]{:S(2)}) async-start(), calls=%async_computation.3 | async-start | bytes 1441792 | tf_op jit(solution)/shard_map/psum | solution.py:139
  17.0 2.5 copy-start.1
  30.2 1.6 copy-start.6
  30.2 2.2 copy-start.7
  32.5 5.7 copy-start.2
  38.2 2.5 copy-start.1
  51.3 1.6 copy-start.6
  51.4 2.2 copy-start.7
  53.6 5.7 copy-start.2
  59.3 2.5 copy-start.1
  72.5 1.6 copy-start.6
  72.5 2.2 copy-start.7
  74.7 5.7 copy-start.2
  80.4 2.5 copy-start.1
  93.6 1.6 copy-start.6
  93.6 2.2 copy-start.7
  95.8 5.7 copy-start.2
  105.2 77.3 %copy-start.3 = (bf16[8,128,128]{2,1,0:T(8,128)(2,1)S(1)}, bf16[8,128,128]{2,1,0:T(8,128)(2,1)}, u32[]{:S(2)}) copy-start(bf16[8,128,128]{2,1,0:T(8,128)(2,1)} %param.11) | copy-start | bytes 786436
  105.2 77.3 %copy-start.5 = (bf16[128,256]{1,0:T(8,128)(2,1)S(1)}, bf16[128,256]{1,0:T(8,128)(2,1)}, u32[]{:S(2)}) copy-start(bf16[128,256]{1,0:T(8,128)(2,1)} %param.14) | copy-start | bytes 196612
  182.8 3.6 collective-permute-start
  184.1 4.8 collective-permute-start.1
  192.7 388.2 %reduce-scatter.2.cloned.1.call-start = ((), (), s32[]{:S(2)}) async-start(), calls=%async_computation.2 | async-start | bytes 2162688 | tf_op jit(solution)/shard_map/reduce_scatter | solution.py:121
  198.3 3.1 copy-start.4
Sparse Core Ops, SparseCore 0:
  192.8 293.4 all-reduce.4
  490.1 90.6 reduce-scatter.1
